TPU v7x, 32 devices: a whole 2x2x4 slice. The times are simulated.
32 devices in a mesh: layer: 16 (over z, x, core), row: 2 (over y).
Axes of the slice: x: 2, y: 2, z: 4, core: 2. Of those that a mesh axis runs over, the one named last changes fastest.
Arguments:
- waves: bfloat16 [16, 3072, 512], P('layer', 'row'), may hold values from -6 to 6
- operators: bfloat16 [16, 4, 3072, 3072], P('layer', None, 'row'), may hold values from -0.0546875 to 0.0546875
- sources: bfloat16 [3072, 512], P('row'), may hold values from -6 to 6
- source_layer: int32 [128], replicated, may hold values from 0 to 15
Outputs:
- traces: bfloat16 [16, 3072, 512], P('layer', 'row')
All inputs are finite; a program needn't handle non-finite values.
Results may differ from a plain program's by a relative error of at most 0.0057.
Values may be sent and summed in bfloat16 or wider, within the bound.
A program may use at most 128 MiB of HBM per device.

v0:
```python
import jax
import jax.numpy as jnp
from jax import lax
from jax.sharding import PartitionSpec as P

TICKS = 3


def shifted(array, axis, by):
    peers = lax.axis_size(axis)
    pairs = [(i, i + by) for i in range(peers) if 0 <= i + by < peers]
    return lax.ppermute(array, axis, pairs)


def combine(real_prod, imag_prod, shot_count):
    real_part = real_prod[:, :shot_count] - imag_prod[:, shot_count:]
    imag_part = real_prod[:, shot_count:] + imag_prod[:, :shot_count]
    return jnp.concatenate([real_part, imag_part], axis=1)


def per_device(waves, operators, sources, source_layer):
    tile_rows = operators.shape[2]
    full_rows = operators.shape[3]
    column_count = waves.shape[2]
    shot_count = column_count // 4
    half = 2 * shot_count
    stacked = operators[0].reshape(4 * tile_rows, full_rows)
    layer_id = lax.axis_index("layer")
    shot_mask = jnp.tile((source_layer == layer_id).astype(jnp.float32), 4)
    source_term = sources.astype(jnp.float32) * shot_mask[None, :]
    current = waves[0]
    for sweep_tick in range(TICKS):
        products = jnp.dot(
            stacked,
            lax.all_gather(current, "row", axis=0, tiled=True),
            preferred_element_type=jnp.float32,
        )
        products = products.reshape(4, tile_rows, column_count)
        down_out = combine(products[0][:, :half], products[1][:, :half], shot_count) + combine(
            products[2][:, half:], products[3][:, half:], shot_count
        )
        up_out = combine(products[0][:, half:], products[1][:, half:], shot_count) + combine(
            products[2][:, :half], products[3][:, :half], shot_count
        )
        down_out = (down_out + source_term[:, :half]).astype(jnp.bfloat16)
        up_out = (up_out + source_term[:, half:]).astype(jnp.bfloat16)
        down_next = shifted(down_out, "layer", 1)
        up_next = shifted(up_out, "layer", -1)
        current = jnp.concatenate([down_next, up_next], axis=1)
    return current[None]


def solution(mesh):
    return jax.shard_map(
        per_device,
        mesh=mesh,
        in_specs=(P("layer", "row", None), P("layer", None, "row", None), P("row", None), P()),
        out_specs=P("layer", "row", None),
        check_vma=False,
    )
```

profile of v0, /device:TPU:9, one launch (start us, length us, event | category | flops | bytes accessed | tf_op | source)
XLA Modules:
  0.0 324.4 jit_solution(11651561303536006612)
XLA Ops:
  6.5 0.7 all-gather.9.cloned.1.call-update
  7.3 0.6 copy-done
  7.9 1.6 copy.5
  9.5 1.7 convert_multiply_fusion
  11.2 43.6 %all-gather.9.cloned.1.call-done = bf16[1,3072,512]{2,1,0:T(8,128)(2,1)} async-done(((bf16[1,1536,512]{2,1,0:T(8,128)(2,1)}), bf16[1,3072,512]{2,1,0:T(8,128)(2,1)}) %all-gather.9.cloned.1.call-update) | async-done | bytes 3145744 | tf_op jit(solution)/shard_map/all_gather | solution.py:35
  54.8 26.8 %fusion = f32[6144,512]{0,1:T(8,128)} fusion(bf16[6144,3072]{1,0:T(8,128)(2,1)} %bitcast.17, bf16[1,3072,512]{2,1,0:T(8,128)(2,1)} %all-gather.9.cloned.1.call-done), kind=kOutput, calls=%fused_computation.2 | convolution fusion | flops 19327352832 | bytes 53477376 | tf_op jit(solution)/shard_map/dot_general | solution.py:33
  81.6 6.0 %slice_subtract_fusion.10 = (f32[1536,128]{0,1:T(8,128)S(1)}, f32[1536,128]{0,1:T(8,128)S(1)}, f32[1536,128]{0,1:T(8,128)S(1)}, f32[1536,128]{0,1:T(8,128)S(1)},...) fusion(f32[6144,512]{0,1:T(8,128)} %fusion), kind=kLoop, calls=%fused_computation.47 | loop fusion | flops 1572864 | bytes 18874368 | tf_op jit(solution)/shard_map/sub | solution.py:16
  87.6 1.1 fusion.3
  88.7 3.8 %collective-permute-start = (bf16[1536,256]{0,1:T(8,128)(2,1)S(1)}, bf16[1536,256]{0,1:T(8,128)(2,1)S(1)}, u32[]{:S(2)}, u32[]{:S(2)}) collective-permute-start(bf16[1536,256]{0,1:T(8,128)(2,1)S(1)} %get-tuple-element.33), channel_id=1, source_target_pairs={{0,2},{2,4},{4,6},{6,8},{8,10},{10,12},{12,14},{14,16},{16,18},{18... | collective-permute-start | bytes 2359304 | tf_op jit(solution)/shard_map/ppermute | solution.py:12
  92.5 1.9 collective-permute-start.1
  94.5 15.4 %collective-permute-done = bf16[1536,256]{0,1:T(8,128)(2,1)S(1)} collective-permute-done((bf16[1536,256]{0,1:T(8,128)(2,1)S(1)}, bf16[1536,256]{0,1:T(8,128)(2,1)S(1)}, u32[]{:S(2)}, u32[]{:S(2)}) %collective-permute-start) | collective-permute-done | bytes 786464 | tf_op jit(solution)/shard_map/ppermute | solution.py:12
  109.9 1.6 collective-permute-done.1
  111.5 1.2 pad_maximum_fusion
  112.8 0.2 all-gather.7.cloned.1.call-start
  113.0 43.2 %all-gather.5.cloned.1.call-done = bf16[3072,512]{0,1:T(8,128)(2,1)} async-done(((bf16[1536,512]{0,1:T(8,128)(2,1)}), bf16[3072,512]{0,1:T(8,128)(2,1)}) %all-gather.5.cloned.1.call-update) | async-done | bytes 3145744 | tf_op jit(solution)/shard_map/all_gather | solution.py:35
  156.3 27.7 %convolution_bitcast_fusion.1 = f32[6144,512]{0,1:T(8,128)} fusion(bf16[3072,512]{0,1:T(8,128)(2,1)} %all-gather.5.cloned.1.call-done, bf16[6144,3072]{1,0:T(8,128)(2,1)} %bitcast.18), kind=kOutput, calls=%fused_computation.1 | convolution fusion | flops 19327352832 | bytes 53477376 | tf_op jit(solution)/shard_map/dot_general | solution.py:33
  184.0 6.0 %slice_subtract_fusion.6 = (f32[1536,128]{0,1:T(8,128)S(1)}, f32[1536,128]{0,1:T(8,128)S(1)}, f32[1536,128]{0,1:T(8,128)S(1)}, f32[1536,128]{0,1:T(8,128)S(1)}, ...) fusion(f32[6144,512]{0,1:T(8,128)} %convolution_bitcast_fusion.1), kind=kLoop, calls=%fused_computation.39 | loop fusion | flops 1572864 | bytes 18874368 | tf_op jit(solution)/shard_map/sub | solution.py:16
  189.9 1.1 fusion.7
  191.1 3.8 %collective-permute-start.2 = (bf16[1536,256]{0,1:T(8,128)(2,1)S(1)}, bf16[1536,256]{0,1:T(8,128)(2,1)S(1)}, u32[]{:S(2)}, u32[]{:S(2)}) collective-permute-start(bf16[1536,256]{0,1:T(8,128)(2,1)S(1)} %get-tuple-element.31), channel_id=1, source_target_pairs={{0,2},{2,4},{4,6},{6,8},{8,10},{10,12},{12,14},{14,16},{16,18},{18... | collective-permute-start | bytes 2359304 | tf_op jit(solution)/shard_map/ppermute | solution.py:12
  194.9 2.1 collective-permute-start.3
  197.1 15.2 %collective-permute-done.2 = bf16[1536,256]{0,1:T(8,128)(2,1)S(1)} collective-permute-done((bf16[1536,256]{0,1:T(8,128)(2,1)S(1)}, bf16[1536,256]{0,1:T(8,128)(2,1)S(1)}, u32[]{:S(2)}, u32[]{:S(2)}) %collective-permute-start.2) | collective-permute-done | bytes 786464 | tf_op jit(solution)/shard_map/ppermute | solution.py:12
  212.3 1.6 collective-permute-done.3
  213.9 1.2 pad_maximum_fusion.1
  215.1 43.5 %all-gather.7.cloned.1.call-done = bf16[3072,512]{0,1:T(8,128)(2,1)} async-done(((bf16[1536,512]{0,1:T(8,128)(2,1)}), bf16[3072,512]{0,1:T(8,128)(2,1)}) %all-gather.7.cloned.1.call-update) | async-done | bytes 3145744 | tf_op jit(solution)/shard_map/all_gather | solution.py:35
  258.6 27.7 %convolution_bitcast_fusion = f32[6144,512]{0,1:T(8,128)} fusion(bf16[3072,512]{0,1:T(8,128)(2,1)} %all-gather.7.cloned.1.call-done, bf16[6144,3072]{1,0:T(8,128)(2,1)} %bitcast.19), kind=kOutput, calls=%fused_computation | convolution fusion | flops 19327352832 | bytes 53477376 | tf_op jit(solution)/shard_map/dot_general | solution.py:33
  286.3 6.0 %slice_subtract_fusion.2 = (f32[1536,128]{0,1:T(8,128)S(1)}, f32[1536,128]{0,1:T(8,128)S(1)}, f32[1536,128]{0,1:T(8,128)S(1)}, f32[1536,128]{0,1:T(8,128)S(1)}, ...) fusion(f32[6144,512]{0,1:T(8,128)} %convolution_bitcast_fusion), kind=kLoop, calls=%fused_computation.31 | loop fusion | flops 1572864 | bytes 18874368 | tf_op jit(solution)/shard_map/sub | solution.py:16
  292.3 1.1 fusion.11
  293.4 3.8 %collective-permute-start.4 = (bf16[1536,256]{0,1:T(8,128)(2,1)S(1)}, bf16[1536,256]{0,1:T(8,128)(2,1)S(1)}, u32[]{:S(2)}, u32[]{:S(2)}) collective-permute-start(bf16[1536,256]{0,1:T(8,128)(2,1)S(1)} %get-tuple-element.29), channel_id=1, source_target_pairs={{0,2},{2,4},{4,6},{6,8},{8,10},{10,12},{12,14},{14,16},{16,18},{18... | collective-permute-start | bytes 2359304 | tf_op jit(solution)/shard_map/ppermute | solution.py:12
  297.3 1.9 collective-permute-start.5
  299.2 15.4 %collective-permute-done.4 = bf16[1536,256]{0,1:T(8,128)(2,1)S(1)} collective-permute-done((bf16[1536,256]{0,1:T(8,128)(2,1)S(1)}, bf16[1536,256]{0,1:T(8,128)(2,1)S(1)}, u32[]{:S(2)}, u32[]{:S(2)}) %collective-permute-start.4) | collective-permute-done | bytes 786464 | tf_op jit(solution)/shard_map/ppermute | solution.py:12
  314.6 1.6 collective-permute-done.5
  316.3 1.6 copy.6
  (10 shorter events, 0.2 us)
Async XLA Ops:
  6.5 1.4 copy-start
  6.5 48.3 %all-gather.9.cloned.1.call-start = ((), (), s32[]{:S(2)}) async-start(), calls=%async_computation.2 | async-start | bytes 4718592 | tf_op jit(solution)/shard_map/all_gather | solution.py:35
  7.3 149.0 %all-gather.5.cloned.1.call-start = ((), (), s32[]{:S(2)}) async-start(), calls=%async_computation | async-start | bytes 4718592 | tf_op jit(solution)/shard_map/all_gather | solution.py:35
  7.9 1.6 copy-start.1
  88.7 21.2 %collective-permute-start = (bf16[1536,256]{0,1:T(8,128)(2,1)S(1)}, bf16[1536,256]{0,1:T(8,128)(2,1)S(1)}, u32[]{:S(2)}, u32[]{:S(2)}) collective-permute-start(bf16[1536,256]{0,1:T(8,128)(2,1)S(1)} %get-tuple-element.33), channel_id=1, source_target_pairs={{0,2},{2,4},{4,6},{6,8},{8,10},{10,12},{12,14},{14,16},{16,18},{18... | collective-permute-start | bytes 2359304 | tf_op jit(solution)/shard_map/ppermute | solution.py:12
  92.5 19.0 %collective-permute-start.1 = (bf16[1536,256]{0,1:T(8,128)(2,1)S(1)}, bf16[1536,256]{0,1:T(8,128)(2,1)S(1)}, u32[]{:S(2)}, u32[]{:S(2)}) collective-permute-start(bf16[1536,256]{0,1:T(8,128)(2,1)S(1)} %get-tuple-element.34), channel_id=1, source_target_pairs={{2,0},{4,2},{6,4},{8,6},{10,8},{12,10},{14,12},{16,14},{18,16},{20... | collective-permute-start | bytes 2359304 | tf_op jit(solution)/shard_map/ppermute | solution.py:12
  112.8 145.8 %all-gather.7.cloned.1.call-start = ((), (), s32[]{:S(2)}) async-start(), calls=%async_computation.1 | async-start | bytes 4718592 | tf_op jit(solution)/shard_map/all_gather | solution.py:35
  191.1 21.2 %collective-permute-start.2 = (bf16[1536,256]{0,1:T(8,128)(2,1)S(1)}, bf16[1536,256]{0,1:T(8,128)(2,1)S(1)}, u32[]{:S(2)}, u32[]{:S(2)}) collective-permute-start(bf16[1536,256]{0,1:T(8,128)(2,1)S(1)} %get-tuple-element.31), channel_id=1, source_target_pairs={{0,2},{2,4},{4,6},{6,8},{8,10},{10,12},{12,14},{14,16},{16,18},{18... | collective-permute-start | bytes 2359304 | tf_op jit(solution)/shard_map/ppermute | solution.py:12
  194.9 19.0 %collective-permute-start.3 = (bf16[1536,256]{0,1:T(8,128)(2,1)S(1)}, bf16[1536,256]{0,1:T(8,128)(2,1)S(1)}, u32[]{:S(2)}, u32[]{:S(2)}) collective-permute-start(bf16[1536,256]{0,1:T(8,128)(2,1)S(1)} %get-tuple-element.32), channel_id=1, source_target_pairs={{2,0},{4,2},{6,4},{8,6},{10,8},{12,10},{14,12},{16,14},{18,16},{20... | collective-permute-start | bytes 2359304 | tf_op jit(solution)/shard_map/ppermute | solution.py:12
  293.4 21.2 %collective-permute-start.4 = (bf16[1536,256]{0,1:T(8,128)(2,1)S(1)}, bf16[1536,256]{0,1:T(8,128)(2,1)S(1)}, u32[]{:S(2)}, u32[]{:S(2)}) collective-permute-start(bf16[1536,256]{0,1:T(8,128)(2,1)S(1)} %get-tuple-element.29), channel_id=1, source_target_pairs={{0,2},{2,4},{4,6},{6,8},{8,10},{10,12},{12,14},{14,16},{16,18},{18... | collective-permute-start | bytes 2359304 | tf_op jit(solution)/shard_map/ppermute | solution.py:12
  297.3 19.0 %collective-permute-start.5 = (bf16[1536,256]{0,1:T(8,128)(2,1)S(1)}, bf16[1536,256]{0,1:T(8,128)(2,1)S(1)}, u32[]{:S(2)}, u32[]{:S(2)}) collective-permute-start(bf16[1536,256]{0,1:T(8,128)(2,1)S(1)} %get-tuple-element.30), channel_id=1, source_target_pairs={{2,0},{4,2},{6,4},{8,6},{10,8},{12,10},{14,12},{16,14},{18,16},{20... | collective-permute-start | bytes 2359304 | tf_op jit(solution)/shard_map/ppermute | solution.py:12
Sparse Core Ops, SparseCore 0:
  8.9 45.8 all-gather.8
  112.9 43.3 all-gather.4
  215.3 43.3 all-gather.6
where the time goes:
time: 325 us; the launch traced here: 324 us
  waiting for transfers between devices  182 us (56%)
  matrix products  82.2 us (25%)
  other arithmetic  25.6 us (8%)
  starting transfers between devices  17.7 us (5%)
  between operations  13.2 us (4%)
  local copies, waits for them, and re-layouts  3.78 us (1%)
    all_gather x3, waiting for transfers between devices, per_device(): lax.all_gather(current, 'row', axis=0, tiled=True)  130 us
    dot_general x3, matrix products, per_device(): jnp.dot(stacked, lax.all_gather(current, 'row', axis=0, tiled=True), pref...  82.2 us
    ppermute x6, waiting for transfers between devices, shifted(): return lax.ppermute(array, axis, pairs)  50.9 us
    sub x3, other arithmetic, combine(): real_part = real_prod[:, :shot_count] - imag_prod[:, shot_count:]  17.9 us
    ppermute x6, starting transfers between devices, shifted(): return lax.ppermute(array, axis, pairs)  17.4 us
  transfers between devices with their start and end apart: 9, of which 9 were waited for; matrix products, arithmetic and copies ran while one was open for 1% of the time, Pallas kernels for 0%

commit v1 on v0

--- a/solution.py
+++ b/solution.py
@@ -32,7 +32,9 @@
     for sweep_tick in range(TICKS):
         products = jnp.dot(
             stacked,
-            lax.all_gather(current, "row", axis=0, tiled=True),
+            jnp.concatenate(
+                lax.all_to_all(jnp.stack([current] * lax.axis_size("row")), "row", 0, 0), axis=0
+            ),
             preferred_element_type=jnp.float32,
         )
         products = products.reshape(4, tile_rows, column_count)

time: 325 us -> 296 us (0.911)
  waiting for transfers between devices: 182 us -> 80.1 us
  blocking collectives: 0 us -> 66.8 us
  between operations: 13.2 us -> 0.14 us
  local copies, waits for them, and re-layouts: 3.78 us -> 12.6 us
  starting transfers between devices: 17.7 us -> 24.9 us
    all_gather x3 -> x0, waiting for transfers between devices: 130 us -> none  [per_device(): lax.all_gather(current, 'row', axis=0, tiled=True)]
    all_to_all x0 -> x2, blocking collectives: none -> 66.8 us  [per_device(): lax.all_to_all(jnp.stack([current] * lax.axis_size('row')), 'row', 0, 0)]
    all_to_all x0 -> x1, waiting for transfers between devices: none -> 32.3 us  [per_device(): lax.all_to_all(jnp.stack([current] * lax.axis_size('row')), 'row', 0, 0)]
    all_to_all x0 -> x2, local copies, waits for them, and re-layouts: none -> 9.48 us  [per_device(): lax.all_to_all(jnp.stack([current] * lax.axis_size('row')), 'row', 0, 0)]
    all_to_all x0 -> x1, starting transfers between devices: none -> 5.35 us  [per_device(): lax.all_to_all(jnp.stack([current] * lax.axis_size('row')), 'row', 0, 0)]
    another operation x0 -> x5, other arithmetic: none -> 4.56 us  [per_device(): jnp.stack([current] * lax.axis_size('row'))]
  transfers between devices with their start and end apart: 9 -> 7, of which waited for: 9 -> 5; matrix products, arithmetic and copies ran while one was open for 1% -> 1% of each run, Pallas kernels for 0% -> 0%
where the time goes in v1:
time: 296 us; the launch traced here: 295 us
  matrix products  82.8 us (28%)
  waiting for transfers between devices  80.1 us (27%)
  blocking collectives  66.8 us (23%)
  other arithmetic  27.7 us (9%)
  starting transfers between devices  24.9 us (8%)
  local copies, waits for them, and re-layouts  12.6 us (4%)
    dot_general x3, matrix products, per_device(): jnp.dot(stacked, jnp.concatenate(lax.all_to_all(jnp.stack([current] * lax...  82.8 us
    all_to_all x2, blocking collectives, per_device(): lax.all_to_all(jnp.stack([current] * lax.axis_size('row')), 'row', 0, 0)  66.8 us
    ppermute x6, waiting for transfers between devices, shifted(): return lax.ppermute(array, axis, pairs)  47.8 us
    all_to_all x1, waiting for transfers between devices, per_device(): lax.all_to_all(jnp.stack([current] * lax.axis_size('row')), 'row', 0, 0)  32.3 us
    ppermute x6, starting transfers between devices, shifted(): return lax.ppermute(array, axis, pairs)  19.5 us
    sub x3, other arithmetic, combine(): real_part = real_prod[:, :shot_count] - imag_prod[:, shot_count:]  17.9 us
    all_to_all x2, local copies, waits for them, and re-layouts, per_device(): lax.all_to_all(jnp.stack([current] * lax.axis_size('row')), 'row', 0, 0)  9.48 us
  transfers between devices with their start and end apart: 7, of which 5 were waited for; matrix products, arithmetic and copies ran while one was open for 1% of the time, Pallas kernels for 0%

profile of v1, /device:TPU:9, one launch (start us, length us, event | category | flops | bytes accessed | tf_op | source)
XLA Modules:
  0.0 295.0 jit_solution(1667937115095855908)
XLA Ops:
  0.0 3.8 %pad_maximum_fusion = bf16[2,1536,512]{2,1,0:T(8,128)(2,1)} fusion(bf16[1,1536,512]{2,1,0:T(8,128)(2,1)} %param.4), kind=kLoop, calls=%fused_computation.3 | loop fusion | flops 1572864 | bytes 4718592 | tf_op jit(solution)/shard_map/stack | solution.py:36
  3.8 5.4 %all-to-all-start = ((bf16[2,1536,512]{2,1,0:T(8,128)(2,1)}), bf16[2,1536,512]{2,1,0:T(8,128)(2,1)}, u32[]{:S(2)}, u32[]{:S(2)}) async-start(bf16[2,1536,512]{2,1,0:T(8,128)(2,1)} %pad_maximum_fusion), calls=%async_computation | async-start | bytes 6291456 | tf_op jit(solution)/shard_map/all_to_all | solution.py:36
  9.2 1.6 copy.7
  10.8 1.7 convert_multiply_fusion
  12.5 32.3 %all-to-all-done = bf16[2,1536,512]{2,1,0:T(8,128)(2,1)} async-done(((bf16[2,1536,512]{2,1,0:T(8,128)(2,1)}), bf16[2,1536,512]{2,1,0:T(8,128)(2,1)}, u32[]{:S(2)}, u32[]{:S(2)}) %all-to-all-start) | async-done | bytes 3145760 | tf_op jit(solution)/shard_map/all_to_all | solution.py:36
  44.8 27.6 %convolution_bitcast_fusion.2 = f32[6144,512]{0,1:T(8,128)} fusion(bf16[3072,512]{1,0:T(8,128)(2,1)} %bitcast, bf16[6144,3072]{1,0:T(8,128)(2,1)} %bitcast.26), kind=kOutput, calls=%fused_computation.2 | convolution fusion | flops 19327352832 | bytes 53477376 | tf_op jit(solution)/shard_map/dot_general | solution.py:33
  72.4 6.0 %slice_subtract_fusion.10 = (f32[1536,128]{0,1:T(8,128)S(1)}, f32[1536,128]{0,1:T(8,128)S(1)}, f32[1536,128]{0,1:T(8,128)S(1)}, f32[1536,128]{0,1:T(8,128)S(1)},...) fusion(f32[6144,512]{0,1:T(8,128)} %convolution_bitcast_fusion.2), kind=kLoop, calls=%fused_computation.49 | loop fusion | flops 1572864 | bytes 18874368 | tf_op jit(solution)/shard_map/sub | solution.py:16
  78.3 1.1 fusion.1
  79.5 4.5 %collective-permute-start = (bf16[1536,256]{0,1:T(8,128)(2,1)S(1)}, bf16[1536,256]{0,1:T(8,128)(2,1)S(1)}, u32[]{:S(2)}, u32[]{:S(2)}) collective-permute-start(bf16[1536,256]{0,1:T(8,128)(2,1)S(1)} %get-tuple-element.33), channel_id=1, source_target_pairs={{0,2},{2,4},{4,6},{6,8},{8,10},{10,12},{12,14},{14,16},{16,18},{18... | collective-permute-start | bytes 2359304 | tf_op jit(solution)/shard_map/ppermute | solution.py:12
  84.0 1.9 collective-permute-start.1
  85.9 15.4 %collective-permute-done = bf16[1536,256]{0,1:T(8,128)(2,1)S(1)} collective-permute-done((bf16[1536,256]{0,1:T(8,128)(2,1)S(1)}, bf16[1536,256]{0,1:T(8,128)(2,1)S(1)}, u32[]{:S(2)}, u32[]{:S(2)}) %collective-permute-start) | collective-permute-done | bytes 786464 | tf_op jit(solution)/shard_map/ppermute | solution.py:12
  101.3 1.6 collective-permute-done.1
  102.9 0.1 maximum_bitcast_fusion
  103.0 0.3 pad_maximum_fusion.1
  103.3 34.4 %all_to_all.15 = bf16[2,1536,512]{1,2,0:T(8,128)(2,1)} all-to-all(bf16[2,1536,512]{1,2,0:T(8,128)(2,1)S(1)} %pad_maximum_fusion.1), channel_id=1, replica_groups=mesh['layer'=16,'row'=2] {'row'}, dimensions={0} | all-to-all | bytes 6291456 | tf_op jit(solution)/shard_map/all_to_all | solution.py:36
  137.8 4.7 %copy.8 = bf16[2,1536,512]{2,1,0:T(8,128)(2,1)} copy(bf16[2,1536,512]{1,2,0:T(8,128)(2,1)} %all_to_all.15) | data formatting | bytes 6291456 | tf_op jit(solution)/shard_map/all_to_all | solution.py:36
  142.5 27.6 %convolution_bitcast_fusion.1 = f32[6144,512]{0,1:T(8,128)} fusion(bf16[3072,512]{1,0:T(8,128)(2,1)} %bitcast.24, bf16[6144,3072]{1,0:T(8,128)(2,1)} %bitcast.27), kind=kOutput, calls=%fused_computation.1 | convolution fusion | flops 19327352832 | bytes 53477376 | tf_op jit(solution)/shard_map/dot_general | solution.py:33
  170.1 6.0 %slice_subtract_fusion.6 = (f32[1536,128]{0,1:T(8,128)S(1)}, f32[1536,128]{0,1:T(8,128)S(1)}, f32[1536,128]{0,1:T(8,128)S(1)}, f32[1536,128]{0,1:T(8,128)S(1)}, ...) fusion(f32[6144,512]{0,1:T(8,128)} %convolution_bitcast_fusion.1), kind=kLoop, calls=%fused_computation.41 | loop fusion | flops 1572864 | bytes 18874368 | tf_op jit(solution)/shard_map/sub | solution.py:16
  176.1 1.1 fusion.5
  177.2 4.6 %collective-permute-start.2 = (bf16[1536,256]{0,1:T(8,128)(2,1)S(1)}, bf16[1536,256]{0,1:T(8,128)(2,1)S(1)}, u32[]{:S(2)}, u32[]{:S(2)}) collective-permute-start(bf16[1536,256]{0,1:T(8,128)(2,1)S(1)} %get-tuple-element.31), channel_id=1, source_target_pairs={{0,2},{2,4},{4,6},{6,8},{8,10},{10,12},{12,14},{14,16},{16,18},{18... | collective-permute-start | bytes 2359304 | tf_op jit(solution)/shard_map/ppermute | solution.py:12
  181.8 1.9 collective-permute-start.3
  183.8 15.4 %collective-permute-done.2 = bf16[1536,256]{0,1:T(8,128)(2,1)S(1)} collective-permute-done((bf16[1536,256]{0,1:T(8,128)(2,1)S(1)}, bf16[1536,256]{0,1:T(8,128)(2,1)S(1)}, u32[]{:S(2)}, u32[]{:S(2)}) %collective-permute-start.2) | collective-permute-done | bytes 786464 | tf_op jit(solution)/shard_map/ppermute | solution.py:12
  199.3 0.3 pad_maximum_fusion.2
  199.6 32.3 %all_to_all.16 = bf16[2,1536,512]{1,2,0:T(8,128)(2,1)} all-to-all(bf16[2,1536,512]{1,2,0:T(8,128)(2,1)S(1)} %pad_maximum_fusion.2), channel_id=1, replica_groups=mesh['layer'=16,'row'=2] {'row'}, dimensions={0} | all-to-all | bytes 6291456 | tf_op jit(solution)/shard_map/all_to_all | solution.py:36
  231.9 4.7 %copy.9 = bf16[2,1536,512]{2,1,0:T(8,128)(2,1)} copy(bf16[2,1536,512]{1,2,0:T(8,128)(2,1)} %all_to_all.16) | data formatting | bytes 6291456 | tf_op jit(solution)/shard_map/all_to_all | solution.py:36
  236.6 27.6 %convolution_bitcast_fusion = f32[6144,512]{0,1:T(8,128)} fusion(bf16[3072,512]{1,0:T(8,128)(2,1)} %bitcast.25, bf16[6144,3072]{1,0:T(8,128)(2,1)} %bitcast.28), kind=kOutput, calls=%fused_computation | convolution fusion | flops 19327352832 | bytes 53477376 | tf_op jit(solution)/shard_map/dot_general | solution.py:33
  264.2 6.0 %slice_subtract_fusion.2 = (f32[1536,128]{0,1:T(8,128)S(1)}, f32[1536,128]{0,1:T(8,128)S(1)}, f32[1536,128]{0,1:T(8,128)S(1)}, f32[1536,128]{0,1:T(8,128)S(1)}, ...) fusion(f32[6144,512]{0,1:T(8,128)} %convolution_bitcast_fusion), kind=kLoop, calls=%fused_computation.33 | loop fusion | flops 1572864 | bytes 18874368 | tf_op jit(solution)/shard_map/sub | solution.py:16
  270.2 1.1 fusion.9
  271.3 4.6 %collective-permute-start.4 = (bf16[1536,256]{0,1:T(8,128)(2,1)S(1)}, bf16[1536,256]{0,1:T(8,128)(2,1)S(1)}, u32[]{:S(2)}, u32[]{:S(2)}) collective-permute-start(bf16[1536,256]{0,1:T(8,128)(2,1)S(1)} %get-tuple-element.29), channel_id=1, source_target_pairs={{0,2},{2,4},{4,6},{6,8},{8,10},{10,12},{12,14},{14,16},{16,18},{18... | collective-permute-start | bytes 2359304 | tf_op jit(solution)/shard_map/ppermute | solution.py:12
  275.9 1.9 collective-permute-start.5
  277.9 15.4 %collective-permute-done.4 = bf16[1536,256]{0,1:T(8,128)(2,1)S(1)} collective-permute-done((bf16[1536,256]{0,1:T(8,128)(2,1)S(1)}, bf16[1536,256]{0,1:T(8,128)(2,1)S(1)}, u32[]{:S(2)}, u32[]{:S(2)}) %collective-permute-start.4) | collective-permute-done | bytes 786464 | tf_op jit(solution)/shard_map/ppermute | solution.py:12
  293.4 1.6 copy.10
  (10 shorter events, 0.2 us)
Async XLA Ops:
  3.8 5.4 %copy-start = (bf16[1536,512]{1,0:T(8,128)(2,1)S(1)}, bf16[1536,512]{1,0:T(8,128)(2,1)}, u32[]{:S(2)}) copy-start(bf16[1536,512]{1,0:T(8,128)(2,1)} %param.6) | copy-start | bytes 4718596
  3.8 40.9 %all-to-all-start = ((bf16[2,1536,512]{2,1,0:T(8,128)(2,1)}), bf16[2,1536,512]{2,1,0:T(8,128)(2,1)}, u32[]{:S(2)}, u32[]{:S(2)}) async-start(bf16[2,1536,512]{2,1,0:T(8,128)(2,1)} %pad_maximum_fusion), calls=%async_computation | async-start | bytes 6291456 | tf_op jit(solution)/shard_map/all_to_all | solution.py:36
  9.2 1.6 copy-start.1
  79.5 21.9 %collective-permute-start = (bf16[1536,256]{0,1:T(8,128)(2,1)S(1)}, bf16[1536,256]{0,1:T(8,128)(2,1)S(1)}, u32[]{:S(2)}, u32[]{:S(2)}) collective-permute-start(bf16[1536,256]{0,1:T(8,128)(2,1)S(1)} %get-tuple-element.33), channel_id=1, source_target_pairs={{0,2},{2,4},{4,6},{6,8},{8,10},{10,12},{12,14},{14,16},{16,18},{18... | collective-permute-start | bytes 2359304 | tf_op jit(solution)/shard_map/ppermute | solution.py:12
  84.0 18.9 %collective-permute-start.1 = (bf16[1536,256]{0,1:T(8,128)(2,1)S(1)}, bf16[1536,256]{0,1:T(8,128)(2,1)S(1)}, u32[]{:S(2)}, u32[]{:S(2)}) collective-permute-start(bf16[1536,256]{0,1:T(8,128)(2,1)S(1)} %get-tuple-element.34), channel_id=1, source_target_pairs={{2,0},{4,2},{6,4},{8,6},{10,8},{12,10},{14,12},{16,14},{18,16},{20... | collective-permute-start | bytes 2359304 | tf_op jit(solution)/shard_map/ppermute | solution.py:12
  177.2 21.9 %collective-permute-start.2 = (bf16[1536,256]{0,1:T(8,128)(2,1)S(1)}, bf16[1536,256]{0,1:T(8,128)(2,1)S(1)}, u32[]{:S(2)}, u32[]{:S(2)}) collective-permute-start(bf16[1536,256]{0,1:T(8,128)(2,1)S(1)} %get-tuple-element.31), channel_id=1, source_target_pairs={{0,2},{2,4},{4,6},{6,8},{8,10},{10,12},{12,14},{14,16},{16,18},{18... | collective-permute-start | bytes 2359304 | tf_op jit(solution)/shard_map/ppermute | solution.py:12
  181.8 17.3 %collective-permute-start.3 = (bf16[1536,256]{0,1:T(8,128)(2,1)S(1)}, bf16[1536,256]{0,1:T(8,128)(2,1)S(1)}, u32[]{:S(2)}, u32[]{:S(2)}) collective-permute-start(bf16[1536,256]{0,1:T(8,128)(2,1)S(1)} %get-tuple-element.32), channel_id=1, source_target_pairs={{2,0},{4,2},{6,4},{8,6},{10,8},{12,10},{14,12},{16,14},{18,16},{20... | collective-permute-start | bytes 2359304 | tf_op jit(solution)/shard_map/ppermute | solution.py:12
  271.3 22.0 %collective-permute-start.4 = (bf16[1536,256]{0,1:T(8,128)(2,1)S(1)}, bf16[1536,256]{0,1:T(8,128)(2,1)S(1)}, u32[]{:S(2)}, u32[]{:S(2)}) collective-permute-start(bf16[1536,256]{0,1:T(8,128)(2,1)S(1)} %get-tuple-element.29), channel_id=1, source_target_pairs={{0,2},{2,4},{4,6},{6,8},{8,10},{10,12},{12,14},{14,16},{16,18},{18... | collective-permute-start | bytes 2359304 | tf_op jit(solution)/shard_map/ppermute | solution.py:12
  275.9 17.3 %collective-permute-start.5 = (bf16[1536,256]{0,1:T(8,128)(2,1)S(1)}, bf16[1536,256]{0,1:T(8,128)(2,1)S(1)}, u32[]{:S(2)}, u32[]{:S(2)}) collective-permute-start(bf16[1536,256]{0,1:T(8,128)(2,1)S(1)} %get-tuple-element.30), channel_id=1, source_target_pairs={{2,0},{4,2},{6,4},{8,6},{10,8},{12,10},{14,12},{16,14},{18,16},{20... | collective-permute-start | bytes 2359304 | tf_op jit(solution)/shard_map/ppermute | solution.py:12
